TPU v7x, 32 devices: a whole 2x2x4 slice. The times are simulated.
32 devices in a mesh: group: 2 (over x), tensor: 8 (over z, y), dp: 2 (over core).
Axes of the slice: x: 2, y: 2, z: 4, core: 2. Of those that a mesh axis runs over, the one named last changes fastest.
Arguments:
- features: bfloat16 [512, 8192], P(('group', 'dp'), 'tensor'), parts along dimension 0, may hold values from -64 to 64
- cotangent: bfloat16 [512, 8192], P(('group', 'dp'), 'tensor'), parts along dimension 0, may hold values from -64 to 64
- token_tenant: int32 [512], P(('group', 'dp')), parts along dimension 0, may hold values from 0 to 15
- owner_device: int32 [32], P('group'), parts along dimension 0, may hold values from 0 to 15, each once
- frozen_weight: bfloat16 [8192, 8192], P('tensor'), may hold values from -0.09375 to 0.09375
- adapter_down: bfloat16 [32, 16, 8192], P('group', None, 'tensor'), parts along dimension 0, may hold values from -0.0625 to 0.0625
- adapter_up: bfloat16 [32, 16, 8192], P('group', None, 'tensor'), parts along dimension 0, may hold values from -0.29882812 to 0.29882812
- momentum_down: float32 [32, 16, 8192], P(('group', 'tensor', 'dp')), parts along dimension 0, may hold values from -12 to 12
- momentum_up: float32 [32, 16, 8192], P(('group', 'tensor', 'dp')), parts along dimension 0, may hold values from -3 to 3
- variance_down: float32 [32, 16, 8192], P(('group', 'tensor', 'dp')), parts along dimension 0, may hold values from 0.3 to 3
- variance_up: float32 [32, 16, 8192], P(('group', 'tensor', 'dp')), parts along dimension 0, may hold values from 0.02 to 0.2
Outputs:
- projected: bfloat16 [512, 8192], P(('group', 'dp'), 'tensor'), parts along dimension 0
- updated_down: bfloat16 [32, 16, 8192], P('group', None, 'tensor'), parts along dimension 0
- updated_up: bfloat16 [32, 16, 8192], P('group', None, 'tensor'), parts along dimension 0
- mean_down: float32 [32, 16, 8192], P(('group', 'tensor', 'dp')), parts along dimension 0
- mean_up: float32 [32, 16, 8192], P(('group', 'tensor', 'dp')), parts along dimension 0
- power_down: float32 [32, 16, 8192], P(('group', 'tensor', 'dp')), parts along dimension 0
- power_up: float32 [32, 16, 8192], P(('group', 'tensor', 'dp')), parts along dimension 0
There are 2 independent parts, one for each index of `group`. A program takes and returns all parts, laid end to end along the dimension named above; an argument that names none is the same for every part. Nothing has to cross between parts.
Inputs may be any that keep to these rules, and one draw needn't show every extreme that they name: Tenant t belongs to the device whose index along tensor+dp (dp fastest) is owner_device[t]; every index appears once.
All inputs are finite; a program needn't handle non-finite values.
Results may differ from a plain program's by a relative error of at most 0.0014.
The roundings to bfloat16 on the way count: a program that leaves them out, or rounds other values in their place, can miss the bound.
Values sent between devices are 32-bit elements; how exact they have to be, the bound alone decides.
A program may use at most 128 MiB of HBM per device.

v0:
```python
import jax
import jax.numpy as jnp
from jax import lax
from jax.sharding import PartitionSpec as P

adapter_scale = 2.0
clip_norm = 12000.0
learn_rate = 0.004
beta_one = 0.9
beta_two = 0.999
adam_eps = 1e-08
correct_one = 1.0 - beta_one**20
correct_two = 1.0 - beta_two**20


def tenant_mask(token_tenant, tenants, lowrank):
    columns = lax.broadcasted_iota(jnp.int32, (1, tenants * lowrank), 1) // lowrank
    return token_tenant[:, None] == columns


def rank_fold(tenants, lowrank):
    row_index = lax.broadcasted_iota(jnp.int32, (tenants * lowrank, lowrank), 0) % lowrank
    col_index = lax.broadcasted_iota(jnp.int32, (tenants * lowrank, lowrank), 1)
    return (row_index == col_index).astype(jnp.float32)


def select_rank(scores, token_mask, folding):
    picked = jnp.where(token_mask, scores, jnp.zeros_like(scores))
    return jnp.dot(
        picked, folding, precision=lax.Precision.HIGHEST, preferred_element_type=jnp.float32
    )


def spread_rank(values, token_mask, tenants):
    scaled = (adapter_scale * values).astype(jnp.bfloat16)
    tiled_rank = jnp.tile(scaled, (1, tenants))
    return jnp.where(token_mask, tiled_rank, jnp.zeros_like(tiled_rank))


def owner_order(owner_device):
    total = owner_device.shape[0]
    slot_index = lax.broadcasted_iota(jnp.int32, (total, total), 0)
    tenant_index = lax.broadcasted_iota(jnp.int32, (total, total), 1)
    return jnp.sum(jnp.where(owner_device[None, :] == slot_index, tenant_index, 0), axis=1)


def adam_step(gradient, factor, moment, square):
    clipped = gradient * factor
    moment_next = beta_one * moment + (1.0 - beta_one) * clipped
    square_next = beta_two * square + (1.0 - beta_two) * clipped * clipped
    change = (
        learn_rate * (moment_next / correct_one) / (jnp.sqrt(square_next / correct_two) + adam_eps)
    )
    return (moment_next, square_next, change)


def frozen_blocks(features, frozen_weight, width_shard, blocks):
    columns = frozen_weight
    columns = columns.reshape(frozen_weight.shape[0], blocks, width_shard)
    return jnp.einsum("ti,ibc->btc", features, columns, preferred_element_type=jnp.float32)


def on_device(
    features,
    cotangent,
    token_tenant,
    owner_device,
    frozen_weight,
    adapter_down,
    adapter_up,
    momentum_down,
    momentum_up,
    variance_down,
    variance_up,
):
    tokens = features.shape[0]
    tenants, lowrank, width_shard = adapter_down.shape
    parts_tensor = lax.axis_size("tensor")
    parts_dp = lax.axis_size("dp")
    token_mask = tenant_mask(token_tenant, tenants, lowrank)
    folding = rank_fold(tenants, lowrank)
    down_flat = adapter_down.reshape(tenants * lowrank, width_shard)
    up_flattened = adapter_up.reshape(tenants * lowrank, width_shard)
    contract = (((1,), (1,)), ((), ()))
    down_part = select_rank(
        lax.dot_general(features, down_flat, contract, preferred_element_type=jnp.float32),
        token_mask,
        folding,
    )
    up_part = select_rank(
        lax.dot_general(cotangent, up_flattened, contract, preferred_element_type=jnp.float32),
        token_mask,
        folding,
    )
    blocks = lax.axis_size("tensor") * tokens // tokens
    result = frozen_blocks(features, frozen_weight, width_shard, blocks)
    frozen_result = lax.psum_scatter(
        result.reshape(blocks * tokens, width_shard), "tensor", scatter_dimension=0, tiled=True
    )
    down_sum, up_sum = lax.psum((down_part, up_part), "tensor")
    down_scattered = spread_rank(down_sum, token_mask, tenants)
    up_scattered = spread_rank(up_sum, token_mask, tenants)
    adapter_result = jnp.dot(down_scattered, up_flattened, preferred_element_type=jnp.float32)
    projected = (frozen_result + adapter_result).astype(jnp.bfloat16)
    outer_product = (((0,), (0,)), ((), ()))
    down_gradient = lax.dot_general(
        up_scattered, features, outer_product, preferred_element_type=jnp.float32
    )
    up_gradient = lax.dot_general(
        down_scattered, cotangent, outer_product, preferred_element_type=jnp.float32
    )
    down_gradient = down_gradient.reshape(tenants, lowrank, width_shard)
    up_gradient = up_gradient.reshape(tenants, lowrank, width_shard)
    slot_tenant = owner_order(owner_device)
    half_index = lax.broadcasted_iota(jnp.int32, (tenants,), 0)
    slot_index = half_index % parts_tensor * parts_dp + half_index // parts_tensor
    half_tenant = jnp.take(slot_tenant, slot_index, axis=0)
    down_halves = jnp.take(down_gradient, half_tenant, axis=0)
    up_halves = jnp.take(up_gradient, half_tenant, axis=0)
    summed = (
        lax.psum_scatter(down_halves, "dp", scatter_dimension=0, tiled=True),
        lax.psum_scatter(up_halves, "dp", scatter_dimension=0, tiled=True),
    )
    own_down, own_up = (
        lax.all_to_all(summed[0], "tensor", split_axis=0, concat_axis=2, tiled=True),
        lax.all_to_all(summed[1], "tensor", split_axis=0, concat_axis=2, tiled=True),
    )
    squares = jnp.sum(own_down * own_down) + jnp.sum(own_up * own_up)
    factor = clip_norm / jnp.maximum(jnp.sqrt(squares), clip_norm)
    mean_down, power_down, change_down = adam_step(own_down, factor, momentum_down, variance_down)
    mean_up, power_up, change_up = adam_step(own_up, factor, momentum_up, variance_up)
    pieces = (
        lax.all_to_all(change_down, ("tensor", "dp"), split_axis=2, concat_axis=0, tiled=True),
        lax.all_to_all(change_up, ("tensor", "dp"), split_axis=2, concat_axis=0, tiled=True),
    )
    joined = (
        lax.all_gather(pieces[0], "dp", axis=2, tiled=True),
        lax.all_gather(pieces[1], "dp", axis=2, tiled=True),
    )
    back_down = jnp.take(joined[0], owner_device, axis=0)
    back_up = jnp.take(joined[1], owner_device, axis=0)
    updated_down = (adapter_down.astype(jnp.float32) - back_down).astype(jnp.bfloat16)
    updated_up = (adapter_up.astype(jnp.float32) - back_up).astype(jnp.bfloat16)
    return (projected, updated_down, updated_up, mean_down, mean_up, power_down, power_up)


def solution(mesh):
    in_specs = (
        P(("group", "dp"), "tensor"),
        P(("group", "dp"), "tensor"),
        P(("group", "dp")),
        P("group"),
        P("tensor", None),
        P("group", None, "tensor"),
        P("group", None, "tensor"),
        P(("group", "tensor", "dp"), None, None),
        P(("group", "tensor", "dp"), None, None),
        P(("group", "tensor", "dp"), None, None),
        P(("group", "tensor", "dp"), None, None),
    )
    out_specs = (
        P(("group", "dp"), "tensor"),
        P("group", None, "tensor"),
        P("group", None, "tensor"),
        P(("group", "tensor", "dp"), None, None),
        P(("group", "tensor", "dp"), None, None),
        P(("group", "tensor", "dp"), None, None),
        P(("group", "tensor", "dp"), None, None),
    )
    return jax.shard_map(
        on_device, mesh=mesh, in_specs=in_specs, out_specs=out_specs, check_vma=False
    )
```

profile of v0, /device:TPU:0, one launch (start us, length us, event | category | flops | bytes accessed | tf_op | source)
XLA Modules:
  0.0 376.7 jit_solution(10851005240872450794)
XLA Ops:
  11.8 38.9 %all-reduce = (f32[128,16]{0,1:T(8,128)S(1)}, f32[128,16]{0,1:T(8,128)S(1)}) all-reduce(f32[128,16]{0,1:T(8,128)S(1)} %fusion.15, f32[128,16]{0,1:T(8,128)S(1)} %fusion.14), channel_id=1, replica_groups=mesh['group'=2,'tensor'=8,'dp'=2] {'tensor'}, use_global_device_ids=true, to_apply=%region_1.2 | all-reduce | flops 4096 | bytes 32768 | tf_op jit(solution)/shard_map/psum | solution.py:100
  57.0 5.0 %reduce-scatter.8.cloned.1.call-done = f32[8,16,1024]{2,1,0:T(8,128)} async-done(((f32[16,16,1024]{2,1,0:T(8,128)}), f32[8,16,1024]{2,1,0:T(8,128)}) %reduce-scatter.8.cloned.1.call-update) | async-done | bytes 524304 | tf_op jit(solution)/shard_map/reduce_scatter | solution.py:122
  62.0 5.8 %all-to-all-start.1 = ((f32[8,16,1024]{2,1,0:T(8,128)}), f32[8,16,1024]{2,1,0:T(8,128)S(1)}, u32[]{:S(2)}, u32[]{:S(2)}) async-start(f32[8,16,1024]{2,1,0:T(8,128)} %reduce-scatter.8.cloned.1.call-done), calls=%async_computation.4 | async-start | bytes 1048576 | tf_op jit(solution)/shard_map/all_to_all | solution.py:126
  67.8 6.0 %reduce-scatter.6.cloned.1.call-done = f32[8,16,1024]{2,1,0:T(8,128)} async-done(((f32[16,16,1024]{2,1,0:T(8,128)}), f32[8,16,1024]{2,1,0:T(8,128)}) %reduce-scatter.6.cloned.1.call-update) | async-done | bytes 524304 | tf_op jit(solution)/shard_map/reduce_scatter | solution.py:121
  73.9 8.9 %all-to-all-done.1 = f32[8,16,1024]{2,1,0:T(8,128)S(1)} async-done(((f32[8,16,1024]{2,1,0:T(8,128)}), f32[8,16,1024]{2,1,0:T(8,128)S(1)}, u32[]{:S(2)}, u32[]{:S(2)}) %all-to-all-start.1) | async-done | bytes 524320 | tf_op jit(solution)/shard_map/all_to_all | solution.py:126
  82.7 3.6 all-to-all-start
  87.1 13.9 %all-to-all-done = f32[8,16,1024]{2,1,0:T(8,128)S(1)} async-done(((f32[8,16,1024]{2,1,0:T(8,128)}), f32[8,16,1024]{2,1,0:T(8,128)S(1)}, u32[]{:S(2)}, u32[]{:S(2)}) %all-to-all-start) | async-done | bytes 524320 | tf_op jit(solution)/shard_map/all_to_all | solution.py:125
  104.5 6.4 %copy.46 = f32[1,16,8192]{1,0,2:T(1,128)} copy(f32[1,16,8192]{2,1,0:T(8,128)S(1)} %get-tuple-element.13) | data formatting | bytes 1048576 | tf_op jit(solution)/shard_map/div | solution.py:52
  111.5 38.4 %reduce.8 = f32[8192,16]{1,0:T(8,128)} reduce(f32[8192,1,16]{2,1,0:T(1,128)} %bitcast.66, f32[]{:T(128)} %broadcast.462), dimensions={1}, to_apply=%bitcast.51.reduce_sub_computation | reduce | bytes 1048580
  149.9 4.2 %reshape.313 = f32[16,1,8192]{2,1,0:T(1,128)} reshape(f32[8192,16]{1,0:T(8,128)} %reduce.8) | data formatting | bytes 1048576
  154.1 3.7 all-to-all-start.2
  158.2 13.9 %all-to-all-done.2 = f32[16,1,8192]{2,1,0:T(1,128)S(1)} async-done(((f32[16,1,8192]{2,1,0:T(1,128)}), f32[16,1,8192]{2,1,0:T(1,128)S(1)}, u32[]{:S(2)}, u32[]{:S(2)}) %all-to-all-start.2) | async-done | bytes 524320 | tf_op jit(solution)/shard_map/all_to_all | solution.py:133
  174.0 9.3 %reshape.314 = f32[8192,1,16]{2,1,0:T(1,128)} reshape(f32[16,8192]{1,0:T(8,128)S(1)} %reduce.9) | data formatting | bytes 1048576
  183.3 3.5 copy.48
  188.2 6.4 %copy.50 = f32[1,16,8192]{1,0,2:T(1,128)} copy(f32[1,16,8192]{2,1,0:T(8,128)S(1)} %get-tuple-element.10) | data formatting | bytes 1048576 | tf_op jit(solution)/shard_map/div | solution.py:52
  194.6 38.4 %reduce.6 = f32[8192,16]{1,0:T(8,128)} reduce(f32[8192,1,16]{2,1,0:T(1,128)} %bitcast.67, f32[]{:T(128)} %broadcast.462), dimensions={1}, to_apply=%bitcast.53.reduce_sub_computation | reduce | bytes 1048580
  233.0 3.5 reshape.315
  236.5 18.4 %all_to_all.54 = f32[16,1,8192]{2,1,0:T(1,128)S(1)} all-to-all(f32[16,1,8192]{2,1,0:T(1,128)S(1)} %reshape.315), channel_id=1, replica_groups=mesh['group'=2,'tensor'=8,'dp'=2] {'tensor','dp'}, dimensions={0} | all-to-all | bytes 1048576 | tf_op jit(solution)/shard_map/all_to_all | solution.py:134
  256.8 9.3 %reshape.316 = f32[8192,1,16]{2,1,0:T(1,128)} reshape(f32[16,8192]{1,0:T(8,128)S(1)} %reduce.7) | data formatting | bytes 1048576
  266.0 3.5 copy.52
  269.6 10.1 %fusion = f32[8,1024,128]{1,2,0:T(8,128)} fusion(bf16[128,8,8,1024]{3,2,1,0:T(8,128)(2,1)} %bitcast.81, bf16[128,1024]{1,0:T(8,128)(2,1)S(1)} %copy-done), kind=kOutput, calls=%fused_computation.5 | convolution fusion | flops 2147483648 | bytes 21233664 | tf_op jit(solution)/shard_map/ti,ibc->btc/dot_general | solution.py:60
  279.9 1.9 gather_fusion.3
  285.1 82.4 %reduce-scatter.4.cloned.1.call-done = f32[128,1024]{1,0:T(8,128)} async-done(((f32[1024,1024]{1,0:T(8,128)}), f32[128,1024]{1,0:T(8,128)}) %reduce-scatter.4.cloned.1.call-update) | async-done | bytes 524304 | tf_op jit(solution)/shard_map/reduce_scatter | solution.py:97
  367.5 2.1 fusion.4
  (76 shorter events, 22.1 us)
Async XLA Ops:
  8.0 1.6 copy-start
  8.0 45.0 %copy-start.3 = (bf16[128,1024]{1,0:T(8,128)(2,1)S(1)}, bf16[128,1024]{1,0:T(8,128)(2,1)}, u32[]{:S(2)}) copy-start(bf16[128,1024]{1,0:T(8,128)(2,1)} %param.14) | copy-start | bytes 786436
  8.0 44.1 %copy-start.9 = (s32[16]{0:T(128)S(1)}, s32[16]{0:T(128)}, u32[]{:S(2)}) copy-start(s32[16]{0:T(128)} %param.16) | copy-start | bytes 196
  8.0 54.0 %reduce-scatter.8.cloned.1.call-start = ((), (), s32[]{:S(2)}) async-start(), calls=%async_computation.9 | async-start | bytes 1572864 | tf_op jit(solution)/shard_map/reduce_scatter | solution.py:122
  56.2 47.1 %copy-start.4 = (f32[1,16,8192]{2,1,0:T(8,128)S(1)}, f32[1,16,8192]{2,1,0:T(8,128)}, u32[]{:S(2)}) copy-start(f32[1,16,8192]{2,1,0:T(8,128)} %param.20) | copy-start | bytes 1572868
  56.2 47.1 %copy-start.5 = (f32[1,16,8192]{2,1,0:T(8,128)S(1)}, f32[1,16,8192]{2,1,0:T(8,128)}, u32[]{:S(2)}) copy-start(f32[1,16,8192]{2,1,0:T(8,128)} %param.22) | copy-start | bytes 1572868
  56.2 17.7 %reduce-scatter.6.cloned.1.call-start = ((), (), s32[]{:S(2)}) async-start(), calls=%async_computation.8 | async-start | bytes 1572864 | tf_op jit(solution)/shard_map/reduce_scatter | solution.py:121
  62.0 20.7 %all-to-all-start.1 = ((f32[8,16,1024]{2,1,0:T(8,128)}), f32[8,16,1024]{2,1,0:T(8,128)S(1)}, u32[]{:S(2)}, u32[]{:S(2)}) async-start(f32[8,16,1024]{2,1,0:T(8,128)} %reduce-scatter.8.cloned.1.call-done), calls=%async_computation.4 | async-start | bytes 1048576 | tf_op jit(solution)/shard_map/all_to_all | solution.py:126
  82.7 18.3 %all-to-all-start = ((f32[8,16,1024]{2,1,0:T(8,128)}), f32[8,16,1024]{2,1,0:T(8,128)S(1)}, u32[]{:S(2)}, u32[]{:S(2)}) async-start(f32[8,16,1024]{2,1,0:T(8,128)} %reduce-scatter.6.cloned.1.call-done), calls=%async_computation.2 | async-start | bytes 1048576 | tf_op jit(solution)/shard_map/all_to_all | solution.py:125
  154.1 18.0 %all-to-all-start.2 = ((f32[16,1,8192]{2,1,0:T(1,128)}), f32[16,1,8192]{2,1,0:T(1,128)S(1)}, u32[]{:S(2)}, u32[]{:S(2)}) async-start(f32[16,1,8192]{2,1,0:T(1,128)} %reshape.313), calls=%async_computation.5 | async-start | bytes 1048576 | tf_op jit(solution)/shard_map/all_to_all | solution.py:133
  157.8 122.0 %all-gather.5.cloned.1.call-start = ((), (), s32[]{:S(2)}) async-start(), calls=%async_computation.10 | async-start | bytes 1572864 | tf_op jit(solution)/shard_map/all_gather | solution.py:137
  174.0 12.9 %copy-start.6 = (f32[1,16,8192]{2,1,0:T(8,128)S(1)}, f32[1,16,8192]{2,1,0:T(8,128)}, u32[]{:S(2)}) copy-start(f32[1,16,8192]{2,1,0:T(8,128)} %param.21) | copy-start | bytes 1572868
  174.0 12.9 %copy-start.7 = (f32[1,16,8192]{2,1,0:T(8,128)S(1)}, f32[1,16,8192]{2,1,0:T(8,128)}, u32[]{:S(2)}) copy-start(f32[1,16,8192]{2,1,0:T(8,128)} %param.23) | copy-start | bytes 1572868
  186.8 95.0 %all-gather.7.cloned.1.call-start = ((), (), s32[]{:S(2)}) async-start(), calls=%async_computation.11 | async-start | bytes 1572864 | tf_op jit(solution)/shard_map/all_gather | solution.py:138
  269.6 97.9 %reduce-scatter.4.cloned.1.call-start = ((), (), s32[]{:S(2)}) async-start(), calls=%async_computation.7 | async-start | bytes 4718592 | tf_op jit(solution)/shard_map/reduce_scatter | solution.py:97
  279.7 3.9 %copy-start.1 = (bf16[16,16,1024]{2,1,0:T(8,128)(2,1)S(1)}, bf16[16,16,1024]{2,1,0:T(8,128)(2,1)}, u32[]{:S(2)}) copy-start(bf16[16,16,1024]{2,1,0:T(8,128)(2,1)} %param.19) | copy-start | bytes 1572868
  279.7 3.9 %copy-start.2 = (bf16[16,16,1024]{2,1,0:T(8,128)(2,1)S(1)}, bf16[16,16,1024]{2,1,0:T(8,128)(2,1)}, u32[]{:S(2)}) copy-start(bf16[16,16,1024]{2,1,0:T(8,128)(2,1)} %param.18) | copy-start | bytes 1572868
  279.9 87.6 %copy-start.8 = (s32[128]{0:T(128)S(1)}, s32[128]{0:T(128)}, u32[]{:S(2)}) copy-start(s32[128]{0:T(128)} %param.15) | copy-start | bytes 1540
Sparse Core Ops, SparseCore 0:
  56.3 5.6 reduce-scatter.7
  64.2 9.5 reduce-scatter.5
  186.9 8.5 all-gather.4
  269.7 8.5 all-gather.6
Sparse Core Ops, SparseCore 1:
  279.9 87.5 reduce-scatter.3
where the time goes:
time: 378 us; the launch traced here: 377 us
  waiting for transfers between devices  131 us (35%)
  other arithmetic  88.7 us (23%)
  blocking collectives  57.2 us (15%)
  local copies, waits for them, and re-layouts  52.8 us (14%)
  between operations  17 us (4%)
  matrix products  16.4 us (4%)
  starting transfers between devices  13.6 us (4%)
    reduce_scatter x1, waiting for transfers between devices, on_device(): lax.psum_scatter(result.reshape(blocks * tokens, width_shard), 'tensor',...  82.4 us
    unnamed x4, other arithmetic  76.9 us
    psum x1, blocking collectives, on_device(): down_sum, up_sum = lax.psum((down_part, up_part), 'tensor')  38.9 us
    unnamed x25, local copies, waits for them, and re-layouts  26.8 us
    all_to_all x1, blocking collectives, on_device(): lax.all_to_all(change_up, ('tensor', 'dp'), split_axis=2, concat_axis=0,...  18.4 us
    all_to_all x1, waiting for transfers between devices, on_device(): lax.all_to_all(summed[0], 'tensor', split_axis=0, concat_axis=2, tiled=True)  13.9 us
    all_to_all x1, waiting for transfers between devices, on_device(): lax.all_to_all(change_down, ('tensor', 'dp'), split_axis=2, concat_axis=0...  13.9 us
    div x2, local copies, waits for them, and re-layouts, adam_step(): learn_rate * (moment_next / correct_one)  12.8 us
  transfers between devices with their start and end apart: 8, of which 6 were waited for; matrix products, arithmetic and copies ran while one was open for 21% of the time, Pallas kernels for 0%

commit v1 on v0

--- a/solution.py
+++ b/solution.py
@@ -131,7 +131,15 @@
     mean_up, power_up, change_up = adam_step(own_up, factor, momentum_up, variance_up)
     pieces = (
         lax.all_to_all(change_down, ("tensor", "dp"), split_axis=2, concat_axis=0, tiled=True),
-        lax.all_to_all(change_up, ("tensor", "dp"), split_axis=2, concat_axis=0, tiled=True),
+        jnp.concatenate(
+            lax.all_to_all(
+                jnp.stack(jnp.split(change_up, lax.axis_size(("tensor", "dp")), axis=2)),
+                ("tensor", "dp"),
+                0,
+                0,
+            ),
+            axis=0,
+        ),
     )
     joined = (
         lax.all_gather(pieces[0], "dp", axis=2, tiled=True),

time: 378 us -> 316 us (0.84)
  other arithmetic: 88.7 us -> 50.2 us
  local copies, waits for them, and re-layouts: 52.8 us -> 30.1 us
    unnamed x4 -> x3, other arithmetic: 76.9 us -> 38.5 us
    unnamed x25 -> x32, local copies, waits for them, and re-layouts: 26.8 us -> 14.1 us
    div x2 -> x1, local copies, waits for them, and re-layouts: 12.8 us -> 6.39 us  [adam_step(): learn_rate * (moment_next / correct_one)]
  transfers between devices with their start and end apart: 8 -> 8, of which waited for: 6 -> 6; matrix products, arithmetic and copies ran while one was open for 21% -> 6% of each run, Pallas kernels for 0% -> 0%
where the time goes in v1:
time: 316 us; the launch traced here: 315 us
  waiting for transfers between devices  130 us (41%)
  blocking collectives  57.3 us (18%)
  other arithmetic  50.2 us (16%)
  local copies, waits for them, and re-layouts  30.1 us (10%)
  matrix products  17.3 us (5%)
  between operations  17 us (5%)
  starting transfers between devices  13.6 us (4%)
    reduce_scatter x1, waiting for transfers between devices, on_device(): lax.psum_scatter(result.reshape(blocks * tokens, width_shard), 'tensor',...  82.4 us
    psum x1, blocking collectives, on_device(): down_sum, up_sum = lax.psum((down_part, up_part), 'tensor')  38.9 us
    unnamed x3, other arithmetic  38.5 us
    all_to_all x1, blocking collectives, on_device(): lax.all_to_all(jnp.stack(jnp.split(change_up, lax.axis_size(('tensor', 'd...  18.5 us
    unnamed x32, local copies, waits for them, and re-layouts  14.1 us
    all_to_all x1, waiting for transfers between devices, on_device(): lax.all_to_all(summed[0], 'tensor', split_axis=0, concat_axis=2, tiled=True)  13.9 us
    all_to_all x1, waiting for transfers between devices, on_device(): lax.all_to_all(change_down, ('tensor', 'dp'), split_axis=2, concat_axis=0...  12.4 us
    dot_general x1, matrix products, frozen_blocks(): jnp.einsum('ti,ibc->btc', features, columns, preferred_element_type=jnp.f...  10.2 us
  transfers between devices with their start and end apart: 8, of which 6 were waited for; matrix products, arithmetic and copies ran while one was open for 6% of the time, Pallas kernels for 0%

profile of v1, /device:TPU:0, one launch (start us, length us, event | category | flops | bytes accessed | tf_op | source)
XLA Modules:
  0.0 315.2 jit_solution(526088851736116084)
XLA Ops:
  8.1 1.4 convolution_select_fusion
  11.7 38.9 %all-reduce = (f32[128,16]{0,1:T(8,128)S(1)}, f32[128,16]{0,1:T(8,128)S(1)}) all-reduce(f32[128,16]{0,1:T(8,128)S(1)} %fusion.15, f32[128,16]{0,1:T(8,128)S(1)} %fusion.14), channel_id=1, replica_groups=mesh['group'=2,'tensor'=8,'dp'=2] {'tensor'}, use_global_device_ids=true, to_apply=%region_1.2 | all-reduce | flops 4096 | bytes 32768 | tf_op jit(solution)/shard_map/psum | solution.py:100
  56.1 1.6 broadcast_select_fusion
  58.5 5.1 %reduce-scatter.8.cloned.1.call-done = f32[8,16,1024]{2,1,0:T(8,128)} async-done(((f32[16,16,1024]{2,1,0:T(8,128)}), f32[8,16,1024]{2,1,0:T(8,128)}) %reduce-scatter.8.cloned.1.call-update) | async-done | bytes 524304 | tf_op jit(solution)/shard_map/reduce_scatter | solution.py:122
  63.5 5.8 %all-to-all-start.1 = ((f32[8,16,1024]{2,1,0:T(8,128)}), f32[8,16,1024]{2,1,0:T(8,128)S(1)}, u32[]{:S(2)}, u32[]{:S(2)}) async-start(f32[8,16,1024]{2,1,0:T(8,128)} %reduce-scatter.8.cloned.1.call-done), calls=%async_computation.4 | async-start | bytes 1048576 | tf_op jit(solution)/shard_map/all_to_all | solution.py:126
  69.3 6.0 %reduce-scatter.6.cloned.1.call-done = f32[8,16,1024]{2,1,0:T(8,128)} async-done(((f32[16,16,1024]{2,1,0:T(8,128)}), f32[8,16,1024]{2,1,0:T(8,128)}) %reduce-scatter.6.cloned.1.call-update) | async-done | bytes 524304 | tf_op jit(solution)/shard_map/reduce_scatter | solution.py:121
  75.4 8.9 %all-to-all-done.1 = f32[8,16,1024]{2,1,0:T(8,128)S(1)} async-done(((f32[8,16,1024]{2,1,0:T(8,128)}), f32[8,16,1024]{2,1,0:T(8,128)S(1)}, u32[]{:S(2)}, u32[]{:S(2)}) %all-to-all-start.1) | async-done | bytes 524320 | tf_op jit(solution)/shard_map/all_to_all | solution.py:126
  84.2 3.6 %all-to-all-start = ((f32[8,16,1024]{2,1,0:T(8,128)}), f32[8,16,1024]{2,1,0:T(8,128)S(1)}, u32[]{:S(2)}, u32[]{:S(2)}) async-start(f32[8,16,1024]{2,1,0:T(8,128)} %reduce-scatter.6.cloned.1.call-done), calls=%async_computation.2 | async-start | bytes 1048576 | tf_op jit(solution)/shard_map/all_to_all | solution.py:125
  88.6 13.9 %all-to-all-done = f32[8,16,1024]{2,1,0:T(8,128)S(1)} async-done(((f32[8,16,1024]{2,1,0:T(8,128)}), f32[8,16,1024]{2,1,0:T(8,128)S(1)}, u32[]{:S(2)}, u32[]{:S(2)}) %all-to-all-start) | async-done | bytes 524320 | tf_op jit(solution)/shard_map/all_to_all | solution.py:125
  104.8 2.5 add_divide_fusion.1
  107.2 6.4 %copy.44 = f32[1,16,8192]{1,0,2:T(1,128)} copy(f32[1,16,8192]{2,1,0:T(8,128)S(1)} %get-tuple-element.13) | data formatting | bytes 1048576 | tf_op jit(solution)/shard_map/div | solution.py:52
  114.2 38.4 %reduce.6 = f32[8192,16]{1,0:T(8,128)} reduce(f32[8192,1,16]{2,1,0:T(1,128)} %bitcast.125, f32[]{:T(128)} %broadcast.462), dimensions={1}, to_apply=%bitcast.113.reduce_sub_computation | reduce | bytes 1048580
  152.6 4.2 %reshape.317 = f32[16,1,8192]{2,1,0:T(1,128)} reshape(f32[8192,16]{1,0:T(8,128)} %reduce.6) | data formatting | bytes 1048576
  156.8 3.7 %all-to-all-start.2 = ((f32[16,1,8192]{2,1,0:T(1,128)}), f32[16,1,8192]{2,1,0:T(1,128)S(1)}, u32[]{:S(2)}, u32[]{:S(2)}) async-start(f32[16,1,8192]{2,1,0:T(1,128)} %reshape.317), calls=%async_computation.5 | async-start | bytes 1048576 | tf_op jit(solution)/shard_map/all_to_all | solution.py:133
  162.3 12.4 %all-to-all-done.2 = f32[16,1,8192]{2,1,0:T(1,128)S(1)} async-done(((f32[16,1,8192]{2,1,0:T(1,128)}), f32[16,1,8192]{2,1,0:T(1,128)S(1)}, u32[]{:S(2)}, u32[]{:S(2)}) %all-to-all-start.2) | async-done | bytes 524320 | tf_op jit(solution)/shard_map/all_to_all | solution.py:133
  174.8 1.9 reduce.7
  176.7 9.3 %reshape.318 = f32[8192,1,16]{2,1,0:T(1,128)} reshape(f32[16,8192]{1,0:T(8,128)S(1)} %reduce.7) | data formatting | bytes 1048576
  186.0 3.5 %copy.46 = f32[1,16,16,512]{3,1,2,0:T(8,128)} copy(f32[1,16,16,512]{1,3,2,0:T(8,128)} %bitcast.124) | data formatting | bytes 1048576 | tf_op jit(solution)/shard_map/all_to_all | solution.py:133
  189.6 18.5 %all_to_all.41 = f32[16,1,16,512]{3,2,1,0:T(8,128)} all-to-all(f32[16,1,16,512]{3,2,1,0:T(8,128)S(1)} %fusion.26), channel_id=1, replica_groups=mesh['group'=2,'tensor'=8,'dp'=2] {'tensor','dp'}, dimensions={0} | all-to-all | bytes 1048576 | tf_op jit(solution)/shard_map/all_to_all | solution.py:135
  208.1 10.2 %fusion = f32[8,1024,128]{1,2,0:T(8,128)} fusion(bf16[128,8,8,1024]{3,2,1,0:T(8,128)(2,1)} %bitcast.138, bf16[128,1024]{1,0:T(8,128)(2,1)S(1)} %copy-done), kind=kOutput, calls=%fused_computation.5 | convolution fusion | flops 2147483648 | bytes 21233664 | tf_op jit(solution)/shard_map/ti,ibc->btc/dot_general | solution.py:60
  218.4 1.8 gather_fusion.3
  220.3 1.8 gather_fusion.4
  223.5 82.4 %reduce-scatter.4.cloned.1.call-done = f32[128,1024]{1,0:T(8,128)} async-done(((f32[1024,1024]{1,0:T(8,128)}), f32[128,1024]{1,0:T(8,128)}) %reduce-scatter.4.cloned.1.call-update) | async-done | bytes 524304 | tf_op jit(solution)/shard_map/reduce_scatter | solution.py:97
  306.0 2.1 fusion.4
  (80 shorter events, 13.8 us)
Async XLA Ops:
  8.0 1.5 copy-start
  8.0 55.5 %reduce-scatter.8.cloned.1.call-start = ((), (), s32[]{:S(2)}) async-start(), calls=%async_computation.9 | async-start | bytes 1572864 | tf_op jit(solution)/shard_map/reduce_scatter | solution.py:122
  57.7 103.2 %copy-start.3 = (f32[1,16,8192]{2,1,0:T(8,128)S(1)}, f32[1,16,8192]{2,1,0:T(8,128)}, u32[]{:S(2)}) copy-start(f32[1,16,8192]{2,1,0:T(8,128)} %param.21) | copy-start | bytes 1572868
  57.7 103.2 %copy-start.4 = (f32[1,16,8192]{2,1,0:T(8,128)S(1)}, f32[1,16,8192]{2,1,0:T(8,128)}, u32[]{:S(2)}) copy-start(f32[1,16,8192]{2,1,0:T(8,128)} %param.23) | copy-start | bytes 1572868
  57.7 17.7 %reduce-scatter.6.cloned.1.call-start = ((), (), s32[]{:S(2)}) async-start(), calls=%async_computation.8 | async-start | bytes 1572864 | tf_op jit(solution)/shard_map/reduce_scatter | solution.py:121
  63.5 20.7 %all-to-all-start.1 = ((f32[8,16,1024]{2,1,0:T(8,128)}), f32[8,16,1024]{2,1,0:T(8,128)S(1)}, u32[]{:S(2)}, u32[]{:S(2)}) async-start(f32[8,16,1024]{2,1,0:T(8,128)} %reduce-scatter.8.cloned.1.call-done), calls=%async_computation.4 | async-start | bytes 1048576 | tf_op jit(solution)/shard_map/all_to_all | solution.py:126
  84.2 18.3 %all-to-all-start = ((f32[8,16,1024]{2,1,0:T(8,128)}), f32[8,16,1024]{2,1,0:T(8,128)S(1)}, u32[]{:S(2)}, u32[]{:S(2)}) async-start(f32[8,16,1024]{2,1,0:T(8,128)} %reduce-scatter.6.cloned.1.call-done), calls=%async_computation.2 | async-start | bytes 1048576 | tf_op jit(solution)/shard_map/all_to_all | solution.py:125
  156.8 18.0 %all-to-all-start.2 = ((f32[16,1,8192]{2,1,0:T(1,128)}), f32[16,1,8192]{2,1,0:T(1,128)S(1)}, u32[]{:S(2)}, u32[]{:S(2)}) async-start(f32[16,1,8192]{2,1,0:T(1,128)} %reshape.317), calls=%async_computation.5 | async-start | bytes 1048576 | tf_op jit(solution)/shard_map/all_to_all | solution.py:133
  160.5 57.9 %all-gather.5.cloned.1.call-start = ((), (), s32[]{:S(2)}) async-start(), calls=%async_computation.10 | async-start | bytes 1572864 | tf_op jit(solution)/shard_map/all_gather | solution.py:145
  186.0 32.3 %copy-start.6 = (s32[16]{0:T(128)S(1)}, s32[16]{0:T(128)}, u32[]{:S(2)}) copy-start(s32[16]{0:T(128)} %param.16) | copy-start | bytes 196
  189.5 32.6 %copy-start.1 = (bf16[16,16,1024]{2,1,0:T(8,128)(2,1)S(1)}, bf16[16,16,1024]{2,1,0:T(8,128)(2,1)}, u32[]{:S(2)}) copy-start(bf16[16,16,1024]{2,1,0:T(8,128)(2,1)} %param.19) | copy-start | bytes 1572868
  189.5 32.7 %copy-start.2 = (bf16[16,16,1024]{2,1,0:T(8,128)(2,1)S(1)}, bf16[16,16,1024]{2,1,0:T(8,128)(2,1)}, u32[]{:S(2)}) copy-start(bf16[16,16,1024]{2,1,0:T(8,128)(2,1)} %param.18) | copy-start | bytes 1572868
  189.5 30.8 %all-gather.7.cloned.1.call-start = ((), (), s32[]{:S(2)}) async-start(), calls=%async_computation.11 | async-start | bytes 1572864 | tf_op jit(solution)/shard_map/all_gather | solution.py:146
  208.1 97.9 %reduce-scatter.4.cloned.1.call-start = ((), (), s32[]{:S(2)}) async-start(), calls=%async_computation.7 | async-start | bytes 4718592 | tf_op jit(solution)/shard_map/reduce_scatter | solution.py:97
  208.1 97.9 %copy-start.5 = (s32[128]{0:T(128)S(1)}, s32[128]{0:T(128)}, u32[]{:S(2)}) copy-start(s32[128]{0:T(128)} %param.15) | copy-start | bytes 1540
Sparse Core Ops, SparseCore 0:
  57.8 5.6 reduce-scatter.7
  65.8 9.5 reduce-scatter.5
  189.6 8.5 all-gather.4
  208.2 8.4 all-gather.6
Sparse Core Ops, SparseCore 1:
  218.4 87.5 reduce-scatter.3
